TPU v7x, 32 devices: a whole 2x2x4 slice. The times are simulated.
32 devices in a mesh: imp: 8 (over z, y), camp: 4 (over x, core).
Axes of the slice: x: 2, y: 2, z: 4, core: 2. Of those that a mesh axis runs over, the one named last changes fastest.
Arguments:
- imp_emb: bfloat16 [16384, 256], P(('imp', 'camp')), may hold values from -512 to 512
- imp_cost: bfloat16 [16384], P(('imp', 'camp')), may hold values from 0.099609375 to 1
- camp_emb: bfloat16 [4096, 256], P(('camp', 'imp')), may hold values from -6 to 6
- prices: bfloat16 [4096], P(('camp', 'imp')), may hold values from -5 to 5
- spend_limits: float32 [4096], P(('camp', 'imp')), may hold values from 3 to 32
- block_lists: int32 [128, 4, 8], P('imp', 'camp'), may hold values from 0 to 7, as said below
- block_counts: int32 [128, 4], P('imp', 'camp'), may hold values from 1 to 8, as said below
Outputs:
- new_prices: float32 [4096], P(('camp', 'imp'))
- row_logz: float32 [16384], P('imp')
Inputs may be any that keep to these rules, and one draw needn't show every extreme that they name: `block_lists`: entries of a list of one tile and owner are distinct block numbers of that owner; slots past the count hold block numbers too, which are ignored. `block_counts`: tile 0 uses all 8 slots of every owner.
All inputs are finite; a program needn't handle non-finite values.
Results may differ from a plain program's by a relative error of at most 0.0003.
Values may be sent and summed in bfloat16 or wider, within the bound.
A program may use at most 64 MiB of HBM per device.

v0:
```python
import jax
import jax.numpy as jnp
from jax import lax
from jax.sharding import PartitionSpec as P

D = 256
BLOCK = 128
SLOTS = 8
GROUP = 4


def merged(array, axis, combine):
    everything = jax.tree.map(lambda part: lax.all_gather(part, axis), array)
    initial = jax.tree.map(lambda part: part[0], everything)

    def step(k, so_far):
        return combine(so_far, jax.tree.map(lambda part: part[k], everything))

    return lax.fori_loop(1, lax.axis_size(axis), step, initial)


def local(imp_emb, imp_cost, camp_emb, prices, spend_limits, block_lists, block_counts):
    scale = 3.0 / jnp.sqrt(jnp.float32(D))
    emb_rows, cost_rows = (
        lax.all_gather(imp_emb, "camp", axis=0, tiled=True),
        lax.all_gather(imp_cost, "camp", axis=0, tiled=True),
    )
    camp_all, price_all = (
        lax.all_gather(camp_emb, "imp", axis=0, tiled=True),
        lax.all_gather(prices, "imp", axis=0, tiled=True),
    )
    own_count = camp_all.shape[0] // BLOCK
    camp_table = camp_all.reshape(own_count, BLOCK, D)
    price_table = price_all.astype(jnp.float32).reshape(own_count, BLOCK)
    lists = block_lists[:, 0, :]
    counts = block_counts[:, 0]
    tiles = lists.shape[0]
    turns = tiles // GROUP
    emb_groups = emb_rows.reshape(turns, GROUP, BLOCK, D)
    cost_groups = cost_rows.astype(jnp.float32).reshape(turns, GROUP, BLOCK)
    list_groups = lists.reshape(turns, GROUP, SLOTS)
    count_groups = counts.reshape(turns, GROUP)

    def scores_of(emb, ids, cnt):
        chosen = camp_table[ids]
        chosen_price = price_table[ids]
        raw = jnp.einsum("gbd,gscd->gbsc", emb, chosen, preferred_element_type=jnp.float32)
        logits = raw * scale - chosen_price[:, None, :, :]
        live = (jnp.arange(SLOTS, dtype=jnp.int32)[None, :] < cnt[:, None])[:, None, :, None]
        return (logits, live)

    def local_both(items):
        emb, ids, cnt = items
        logits, live = scores_of(emb, ids, cnt)
        top_here = jnp.max(jnp.where(live, logits, -jnp.inf), axis=(2, 3))
        expo = jnp.exp(jnp.where(live, logits - top_here[:, :, None, None], -jnp.inf))
        return (top_here, jnp.sum(expo, axis=(2, 3)))

    tops_here, totals_here = lax.map(local_both, (emb_groups, list_groups, count_groups))

    def combine(first, second):
        larger = jnp.maximum(first[0], second[0])
        summed = first[1] * jnp.exp(first[0] - larger) + second[1] * jnp.exp(second[0] - larger)
        return (larger, summed)

    top, total = merged((tops_here, totals_here), "camp", combine)
    row_logz = (top + jnp.log(total)).reshape(tiles * BLOCK)
    block_index = jnp.arange(own_count, dtype=jnp.int32)

    def accumulate(spend, items):
        emb, ids, cnt, cost, top_now, total_now = items
        logits, live = scores_of(emb, ids, cnt)
        expo = jnp.exp(jnp.where(live, logits - top_now[:, :, None, None], -jnp.inf))
        weight = expo / total_now[:, :, None, None]
        contrib = jnp.sum(weight * cost[:, :, None, None], axis=1)
        slot_live = jnp.arange(SLOTS, dtype=jnp.int32)[None, :] < cnt[:, None]
        onehot = ((ids[:, :, None] == block_index[None, None, :]) & slot_live[:, :, None]).astype(
            jnp.float32
        )
        added = jnp.einsum("gso,gsc->oc", onehot, contrib, precision=lax.Precision.HIGHEST)
        return (spend + added, None)

    spend_zero = jnp.zeros((own_count, BLOCK), jnp.float32)
    spend, unused = lax.scan(
        accumulate, spend_zero, (emb_groups, list_groups, count_groups, cost_groups, top, total)
    )
    spend = spend.reshape(own_count * BLOCK)
    width = prices.shape[0]
    whole = lax.psum(spend, "imp")
    mine = lax.dynamic_slice_in_dim(whole, lax.axis_index("imp") * width, width)
    new_prices = prices.astype(jnp.float32) + 2.0 * (mine - spend_limits) / (mine + spend_limits)
    return (new_prices, row_logz)


def solution(mesh):
    return jax.shard_map(
        local,
        mesh=mesh,
        in_specs=(
            P(("imp", "camp"), None),
            P(("imp", "camp")),
            P(("camp", "imp"), None),
            P(("camp", "imp")),
            P(("camp", "imp")),
            P("imp", "camp", None),
            P("imp", "camp"),
        ),
        out_specs=(P(("camp", "imp")), P("imp")),
        check_vma=False,
    )
```

profile of v0, /device:TPU:0, one launch (start us, length us, event | category | flops | bytes accessed | tf_op | source)
XLA Modules:
  0.0 137.3 jit_solution(15288913521605371296)
XLA Ops:
  7.2 0.7 all-gather.6.cloned.1.call-update
  7.9 0.8 copy.12
  8.7 22.5 %all-gather.2 = bf16[8,1,128]{2,1,0:T(2,128)(2,1)S(1)} all-gather(bf16[1,1,128]{2,1,0:T(2,128)(2,1)} %bitcast.128), channel_id=1, replica_groups=mesh['imp'=8,'camp'=4] {'imp'}, dimensions={0}, use_global_device_ids=true | all-gather | bytes 2304 | tf_op jit(solution)/shard_map/all_gather | solution.py:30
  31.1 0.5 broadcast.122
  31.7 1.2 reduce.3
  33.0 0.7 reshape.223
  33.7 5.2 %all-gather.3 = bf16[4,1,512]{2,1,0:T(2,128)(2,1)S(1)} all-gather(bf16[1,1,512]{2,1,0:T(2,128)(2,1)S(1)} %reshape.223), channel_id=1, replica_groups=mesh['imp'=8,'camp'=4] {'camp'}, dimensions={0}, use_global_device_ids=true | all-gather | bytes 5120 | tf_op jit(solution)/shard_map/all_gather | solution.py:26
  38.9 31.4 %all_gather.25 = bf16[1024,256]{1,0:T(8,128)(2,1)S(1)} all-gather(bf16[128,256]{1,0:T(8,128)(2,1)} %param.15), channel_id=1, replica_groups=mesh['imp'=8,'camp'=4] {'imp'}, dimensions={0}, use_global_device_ids=true | all-gather | bytes 589824 | tf_op jit(solution)/shard_map/all_gather | solution.py:29
  70.3 16.5 %while.40 = (s32[]{:T(128)}, f32[4,4,128]{2,1,0:T(4,128)S(1)}, f32[4,4,128]{2,1,0:T(4,128)S(1)}, s32[4,4]{1,0:T(4,128)S(1)}, bf16[4,4,128,256]{3,2,1,0:T(8,128)(...) while((s32[]{:T(128)}, f32[4,4,128]{2,1,0:T(4,128)S(1)}, ...), condition=%wide.region_3.4_spmd, body=%wide.region_0.3_spmd.sunk | while | flops 273154176 | bytes 10833529 | solution.py:59
  70.4 0.6 gather_fusion
  71.0 0.7 gather_fusion.1
  71.7 1.9 %select_reduce_fusion.2 = (f32[4,128]{1,0:T(4,128)S(1)}, f32[4,128,8,128]{1,3,2,0:T(8,128)S(1)}) fusion(f32[4,8,128]{2,1,0:T(8,128)S(1)} %bitcast.117, pred[4,8]{1,0:T(4,128)(4,1)S(1)} %iota_compare_fusion.5, bf16[4,8,128,256]{3,2,1,0:T(8,128)(2,1)S(1)} %bitcast.116, bf16[4,4,128,256]{3,2,1,0:T(8,128)(2,1)} %get-tuple-element.508, ...), kind=kOutput, calls=%fused_computation.11.clone.1 | convolution fusion | flops 270532096 | bytes 4475424 | tf_op jit(solution)/shard_map/while/body/eval_jaxpr/gbd,gscd->gbsc/dot_general | solution.py:47
  73.6 0.8 exponential_reduce_fusion.2
  74.5 0.6 gather_fusion
  75.1 0.7 gather_fusion.1
  75.9 1.9 %select_reduce_fusion.2 = (f32[4,128]{1,0:T(4,128)S(1)}, f32[4,128,8,128]{1,3,2,0:T(8,128)S(1)}) fusion(f32[4,8,128]{2,1,0:T(8,128)S(1)} %bitcast.117, pred[4,8]{1,0:T(4,128)(4,1)S(1)} %iota_compare_fusion.5, bf16[4,8,128,256]{3,2,1,0:T(8,128)(2,1)S(1)} %bitcast.116, bf16[4,4,128,256]{3,2,1,0:T(8,128)(2,1)} %get-tuple-element.508, ...), kind=kOutput, calls=%fused_computation.11.clone.1 | convolution fusion | flops 270532096 | bytes 4475424 | tf_op jit(solution)/shard_map/while/body/eval_jaxpr/gbd,gscd->gbsc/dot_general | solution.py:47
  77.7 0.8 exponential_reduce_fusion.2
  78.7 0.6 gather_fusion
  79.2 0.7 gather_fusion.1
  80.0 1.9 %select_reduce_fusion.2 = (f32[4,128]{1,0:T(4,128)S(1)}, f32[4,128,8,128]{1,3,2,0:T(8,128)S(1)}) fusion(f32[4,8,128]{2,1,0:T(8,128)S(1)} %bitcast.117, pred[4,8]{1,0:T(4,128)(4,1)S(1)} %iota_compare_fusion.5, bf16[4,8,128,256]{3,2,1,0:T(8,128)(2,1)S(1)} %bitcast.116, bf16[4,4,128,256]{3,2,1,0:T(8,128)(2,1)} %get-tuple-element.508, ...), kind=kOutput, calls=%fused_computation.11.clone.1 | convolution fusion | flops 270532096 | bytes 4475424 | tf_op jit(solution)/shard_map/while/body/eval_jaxpr/gbd,gscd->gbsc/dot_general | solution.py:47
  81.9 0.8 exponential_reduce_fusion.2
  82.8 0.6 gather_fusion
  83.4 0.7 gather_fusion.1
  84.1 1.9 %select_reduce_fusion.2 = (f32[4,128]{1,0:T(4,128)S(1)}, f32[4,128,8,128]{1,3,2,0:T(8,128)S(1)}) fusion(f32[4,8,128]{2,1,0:T(8,128)S(1)} %bitcast.117, pred[4,8]{1,0:T(4,128)(4,1)S(1)} %iota_compare_fusion.5, bf16[4,8,128,256]{3,2,1,0:T(8,128)(2,1)S(1)} %bitcast.116, bf16[4,4,128,256]{3,2,1,0:T(8,128)(2,1)} %get-tuple-element.508, ...), kind=kOutput, calls=%fused_computation.11.clone.1 | convolution fusion | flops 270532096 | bytes 4475424 | tf_op jit(solution)/shard_map/while/body/eval_jaxpr/gbd,gscd->gbsc/dot_general | solution.py:47
  86.0 0.8 exponential_reduce_fusion.2
  86.8 5.2 %all-gather = f32[16,4,128]{2,1,0:T(4,128)S(1)} all-gather(f32[4,4,128]{2,1,0:T(4,128)S(1)} %get-tuple-element.235), channel_id=2, replica_groups=mesh['imp'=8,'camp'=4] {'camp'}, dimensions={0}, use_global_device_ids=true | all-gather | bytes 40960 | tf_op jit(solution)/shard_map/all_gather | solution.py:13
  92.0 5.2 %all-gather.1 = f32[16,4,128]{2,1,0:T(4,128)S(1)} all-gather(f32[4,4,128]{2,1,0:T(4,128)S(1)} %get-tuple-element.236), channel_id=3, replica_groups=mesh['imp'=8,'camp'=4] {'camp'}, dimensions={0}, use_global_device_ids=true | all-gather | bytes 40960 | tf_op jit(solution)/shard_map/all_gather | solution.py:13
  97.2 0.1 while.41
  97.3 14.7 %while.42 = (s32[]{:T(128)}, f32[8,128]{1,0:T(8,128)S(1)}, s32[4,4,8]{2,1,0:T(4,128)S(1)}, s32[4,4]{1,0:T(4,128)S(1)}, bf16[4,4,128,256]{3,2,1,0:T(8,128)(2,1)},...) while((s32[]{:T(128)}, f32[8,128]{1,0:T(8,128)S(1)}, ...), condition=%wide.region_8.9_spmd.clone, body=%wide.region_6.8_spmd.clone.sunk | while | flops 272498304 | bytes 6668323 | solution.py:84
  97.5 0.7 gather_fusion.2
  98.2 0.6 gather_fusion.3
  98.8 2.0 %multiply_reduce_fusion.2 = f32[4,8,128]{2,1,0:T(8,128)S(1)} fusion(bf16[4,8,128,256]{3,2,1,0:T(8,128)(2,1)S(1)} %bitcast.115, f32[4,128]{1,0:T(4,128)S(1)} %get-tuple-element.484, f32[4,128]{1,0:T(4,128)S(1)} %get-tuple-element.485, f32[4,128]{1,0:T(4,128)S(1)} %dynamic-slice_bitcast_fusion.8, f32[4,8,128]{2,1,0:T(8,128)S(1)} %bitcast.121, ...), kind=kOutput, calls=%fused_computation.24.clone.1 | convolution fusion | flops 272101376 | bytes 2398752 | tf_op jit(solution)/shard_map/while/body/eval_jaxpr/gbd,gscd->gbsc/dot_general | solution.py:47
  100.8 0.2 fusion.38
  101.1 0.7 gather_fusion.2
  101.8 0.6 gather_fusion.3
  102.5 2.0 %multiply_reduce_fusion.2 = f32[4,8,128]{2,1,0:T(8,128)S(1)} fusion(bf16[4,8,128,256]{3,2,1,0:T(8,128)(2,1)S(1)} %bitcast.115, f32[4,128]{1,0:T(4,128)S(1)} %get-tuple-element.484, f32[4,128]{1,0:T(4,128)S(1)} %get-tuple-element.485, f32[4,128]{1,0:T(4,128)S(1)} %dynamic-slice_bitcast_fusion.8, f32[4,8,128]{2,1,0:T(8,128)S(1)} %bitcast.121, ...), kind=kOutput, calls=%fused_computation.24.clone.1 | convolution fusion | flops 272101376 | bytes 2398752 | tf_op jit(solution)/shard_map/while/body/eval_jaxpr/gbd,gscd->gbsc/dot_general | solution.py:47
  104.5 0.2 fusion.38
  104.8 0.7 gather_fusion.2
  105.5 0.6 gather_fusion.3
  106.2 2.0 %multiply_reduce_fusion.2 = f32[4,8,128]{2,1,0:T(8,128)S(1)} fusion(bf16[4,8,128,256]{3,2,1,0:T(8,128)(2,1)S(1)} %bitcast.115, f32[4,128]{1,0:T(4,128)S(1)} %get-tuple-element.484, f32[4,128]{1,0:T(4,128)S(1)} %get-tuple-element.485, f32[4,128]{1,0:T(4,128)S(1)} %dynamic-slice_bitcast_fusion.8, f32[4,8,128]{2,1,0:T(8,128)S(1)} %bitcast.121, ...), kind=kOutput, calls=%fused_computation.24.clone.1 | convolution fusion | flops 272101376 | bytes 2398752 | tf_op jit(solution)/shard_map/while/body/eval_jaxpr/gbd,gscd->gbsc/dot_general | solution.py:47
  108.2 0.2 fusion.38
  108.5 0.7 gather_fusion.2
  109.2 0.6 gather_fusion.3
  109.9 2.0 %multiply_reduce_fusion.2 = f32[4,8,128]{2,1,0:T(8,128)S(1)} fusion(bf16[4,8,128,256]{3,2,1,0:T(8,128)(2,1)S(1)} %bitcast.115, f32[4,128]{1,0:T(4,128)S(1)} %get-tuple-element.484, f32[4,128]{1,0:T(4,128)S(1)} %get-tuple-element.485, f32[4,128]{1,0:T(4,128)S(1)} %dynamic-slice_bitcast_fusion.8, f32[4,8,128]{2,1,0:T(8,128)S(1)} %bitcast.121, ...), kind=kOutput, calls=%fused_computation.24.clone.1 | convolution fusion | flops 272101376 | bytes 2398752 | tf_op jit(solution)/shard_map/while/body/eval_jaxpr/gbd,gscd->gbsc/dot_general | solution.py:47
  111.9 0.2 fusion.38
  112.1 17.2 %psum.7 = f32[1024]{0:T(1024)S(1)} all-reduce(f32[1024]{0:T(1024)S(1)} %bitcast.125), channel_id=1, replica_groups=mesh['imp'=8,'camp'=4] {'imp'}, use_global_device_ids=true, to_apply=%region_9.10 | all-reduce | flops 1024 | bytes 8192 | tf_op jit(solution)/shard_map/psum | solution.py:89
  129.3 0.6 log_add_fusion
  129.9 0.6 divide_add_fusion
  (73 shorter events, 1.9 us)
Async XLA Ops:
  7.2 63.1 %all-gather.6.cloned.1.call-start = ((), (), s32[]{:S(2)}) async-start(), calls=%async_computation | async-start | bytes 1310720 | tf_op jit(solution)/shard_map/all_gather | solution.py:25
  97.3 32.6 %copy-start = (bf16[128]{0:T(256)(128)(2,1)S(1)}, bf16[128]{0:T(256)(128)(2,1)}, u32[]{:S(2)}) copy-start(bf16[128]{0:T(256)(128)(2,1)} %param.16) | copy-start | bytes 772
  97.3 32.6 %copy-start.1 = (f32[128]{0:T(128)S(1)}, f32[128]{0:T(128)}, u32[]{:S(2)}) copy-start(f32[128]{0:T(128)} %param.17) | copy-start | bytes 1540
Sparse Core Ops, SparseCore 0:
  9.5 19.4 all-gather.5
where the time goes:
time: 138 us; the launch traced here: 137 us
  blocking collectives  86.6 us (63%)
  matrix products  16 us (12%)
  between operations  14.1 us (10%)
  local copies, waits for them, and re-layouts  13 us (9%)
  other arithmetic  6.35 us (5%)
    all_gather x1, blocking collectives, local(): lax.all_gather(camp_emb, 'imp', axis=0, tiled=True)  31.4 us
    all_gather x1, blocking collectives, local(): lax.all_gather(prices, 'imp', axis=0, tiled=True)  22.5 us
    psum x1, blocking collectives, local(): whole = lax.psum(spend, 'imp')  17.2 us
    dot_general x8, matrix products, scores_of(): jnp.einsum('gbd,gscd->gbsc', emb, chosen, preferred_element_type=jnp.floa...  15.3 us
    all_gather x2, blocking collectives, merged(): everything = jax.tree.map(lambda part: lax.all_gather(part, axis), array)  10.4 us
    gather x8, local copies, waits for them, and re-layouts, scores_of(): chosen = camp_table[ids]  5.48 us
    all_gather x1, blocking collectives, local(): lax.all_gather(imp_cost, 'camp', axis=0, tiled=True)  5.18 us
    gather x8, local copies, waits for them, and re-layouts, scores_of(): chosen_price = price_table[ids]  4.59 us
  transfers between devices with their start and end apart: 1, of which 0 were waited for; matrix products, arithmetic and copies ran while one was open for 2% of the time, Pallas kernels for 0%

commit v1 on v0

--- a/solution.py
+++ b/solution.py
@@ -86,7 +86,7 @@
     )
     spend = spend.reshape(own_count * BLOCK)
     width = prices.shape[0]
-    whole = lax.psum(spend, "imp")
+    whole = jnp.sum(lax.all_gather(spend, "imp"), axis=0)
     mine = lax.dynamic_slice_in_dim(whole, lax.axis_index("imp") * width, width)
     new_prices = prices.astype(jnp.float32) + 2.0 * (mine - spend_limits) / (mine + spend_limits)
     return (new_prices, row_logz)

time: 138 us -> 151 us (1.094)
  blocking collectives: 86.6 us -> 100 us
    all_gather x0 -> x1, blocking collectives: none -> 30.6 us  [local(): whole = jnp.sum(lax.all_gather(spend, 'imp'), axis=0)]
    psum x1 -> x0, blocking collectives: 17.2 us -> none  [local(): whole = lax.psum(spend, 'imp')]
where the time goes in v1:
time: 151 us
  blocking collectives  100 us (66%)
  matrix products  16 us (11%)
  between operations  14.1 us (9%)
  local copies, waits for them, and re-layouts  13 us (9%)
  other arithmetic  6.38 us (4%)
    all_gather x1, blocking collectives, local(): lax.all_gather(camp_emb, 'imp', axis=0, tiled=True)  31.4 us
    all_gather x1, blocking collectives, local(): whole = jnp.sum(lax.all_gather(spend, 'imp'), axis=0)  30.6 us
    all_gather x1, blocking collectives, local(): lax.all_gather(prices, 'imp', axis=0, tiled=True)  22.5 us
    dot_general x8, matrix products, scores_of(): jnp.einsum('gbd,gscd->gbsc', emb, chosen, preferred_element_type=jnp.floa...  15.3 us
    all_gather x2, blocking collectives, merged(): everything = jax.tree.map(lambda part: lax.all_gather(part, axis), array)  10.4 us
    gather x8, local copies, waits for them, and re-layouts, scores_of(): chosen = camp_table[ids]  5.48 us
    all_gather x1, blocking collectives, local(): lax.all_gather(imp_cost, 'camp', axis=0, tiled=True)  5.18 us
    gather x8, local copies, waits for them, and re-layouts, scores_of(): chosen_price = price_table[ids]  4.59 us
  transfers between devices with their start and end apart: 1, of which 0 were waited for; matrix products, arithmetic and copies ran while one was open for 2% of the time, Pallas kernels for 0%

profile of v1, /device:TPU:0, one launch (start us, length us, event | category | flops | bytes accessed | tf_op | source)
XLA Modules:
  0.0 150.8 jit_solution(18296649234135133418)
XLA Ops:
  7.2 0.7 all-gather.7.cloned.1.call-update
  7.9 0.8 copy.12
  8.7 22.5 %all-gather.2 = bf16[8,1,128]{2,1,0:T(2,128)(2,1)S(1)} all-gather(bf16[1,1,128]{2,1,0:T(2,128)(2,1)} %bitcast.128), channel_id=1, replica_groups=mesh['imp'=8,'camp'=4] {'imp'}, dimensions={0}, use_global_device_ids=true | all-gather | bytes 2304 | tf_op jit(solution)/shard_map/all_gather | solution.py:30
  31.1 0.5 broadcast.122
  31.7 1.2 reduce.4
  33.0 0.7 reshape.219
  33.7 5.2 %all-gather.3 = bf16[4,1,512]{2,1,0:T(2,128)(2,1)S(1)} all-gather(bf16[1,1,512]{2,1,0:T(2,128)(2,1)S(1)} %reshape.219), channel_id=1, replica_groups=mesh['imp'=8,'camp'=4] {'camp'}, dimensions={0}, use_global_device_ids=true | all-gather | bytes 5120 | tf_op jit(solution)/shard_map/all_gather | solution.py:26
  38.9 31.4 %all_gather.28 = bf16[1024,256]{1,0:T(8,128)(2,1)S(1)} all-gather(bf16[128,256]{1,0:T(8,128)(2,1)} %param.15), channel_id=1, replica_groups=mesh['imp'=8,'camp'=4] {'imp'}, dimensions={0}, use_global_device_ids=true | all-gather | bytes 589824 | tf_op jit(solution)/shard_map/all_gather | solution.py:29
  70.3 16.5 %while.40 = (s32[]{:T(128)}, f32[4,4,128]{2,1,0:T(4,128)S(1)}, f32[4,4,128]{2,1,0:T(4,128)S(1)}, s32[4,4]{1,0:T(4,128)S(1)}, bf16[4,4,128,256]{3,2,1,0:T(8,128)(...) while((s32[]{:T(128)}, f32[4,4,128]{2,1,0:T(4,128)S(1)}, ...), condition=%wide.region_3.4_spmd, body=%wide.region_0.3_spmd.sunk | while | flops 273154176 | bytes 10833529 | solution.py:59
  70.4 0.6 gather_fusion
  71.0 0.7 gather_fusion.1
  71.7 1.9 %select_reduce_fusion.2 = (f32[4,128]{1,0:T(4,128)S(1)}, f32[4,128,8,128]{1,3,2,0:T(8,128)S(1)}) fusion(f32[4,8,128]{2,1,0:T(8,128)S(1)} %bitcast.117, pred[4,8]{1,0:T(4,128)(4,1)S(1)} %iota_compare_fusion.5, bf16[4,8,128,256]{3,2,1,0:T(8,128)(2,1)S(1)} %bitcast.116, bf16[4,4,128,256]{3,2,1,0:T(8,128)(2,1)} %get-tuple-element.508, ...), kind=kOutput, calls=%fused_computation.11.clone.1 | convolution fusion | flops 270532096 | bytes 4475424 | tf_op jit(solution)/shard_map/while/body/eval_jaxpr/gbd,gscd->gbsc/dot_general | solution.py:47
  73.6 0.8 exponential_reduce_fusion.2
  74.5 0.6 gather_fusion
  75.1 0.7 gather_fusion.1
  75.9 1.9 %select_reduce_fusion.2 = (f32[4,128]{1,0:T(4,128)S(1)}, f32[4,128,8,128]{1,3,2,0:T(8,128)S(1)}) fusion(f32[4,8,128]{2,1,0:T(8,128)S(1)} %bitcast.117, pred[4,8]{1,0:T(4,128)(4,1)S(1)} %iota_compare_fusion.5, bf16[4,8,128,256]{3,2,1,0:T(8,128)(2,1)S(1)} %bitcast.116, bf16[4,4,128,256]{3,2,1,0:T(8,128)(2,1)} %get-tuple-element.508, ...), kind=kOutput, calls=%fused_computation.11.clone.1 | convolution fusion | flops 270532096 | bytes 4475424 | tf_op jit(solution)/shard_map/while/body/eval_jaxpr/gbd,gscd->gbsc/dot_general | solution.py:47
  77.7 0.8 exponential_reduce_fusion.2
  78.7 0.6 gather_fusion
  79.2 0.7 gather_fusion.1
  80.0 1.9 %select_reduce_fusion.2 = (f32[4,128]{1,0:T(4,128)S(1)}, f32[4,128,8,128]{1,3,2,0:T(8,128)S(1)}) fusion(f32[4,8,128]{2,1,0:T(8,128)S(1)} %bitcast.117, pred[4,8]{1,0:T(4,128)(4,1)S(1)} %iota_compare_fusion.5, bf16[4,8,128,256]{3,2,1,0:T(8,128)(2,1)S(1)} %bitcast.116, bf16[4,4,128,256]{3,2,1,0:T(8,128)(2,1)} %get-tuple-element.508, ...), kind=kOutput, calls=%fused_computation.11.clone.1 | convolution fusion | flops 270532096 | bytes 4475424 | tf_op jit(solution)/shard_map/while/body/eval_jaxpr/gbd,gscd->gbsc/dot_general | solution.py:47
  81.9 0.8 exponential_reduce_fusion.2
  82.8 0.6 gather_fusion
  83.4 0.7 gather_fusion.1
  84.1 1.9 %select_reduce_fusion.2 = (f32[4,128]{1,0:T(4,128)S(1)}, f32[4,128,8,128]{1,3,2,0:T(8,128)S(1)}) fusion(f32[4,8,128]{2,1,0:T(8,128)S(1)} %bitcast.117, pred[4,8]{1,0:T(4,128)(4,1)S(1)} %iota_compare_fusion.5, bf16[4,8,128,256]{3,2,1,0:T(8,128)(2,1)S(1)} %bitcast.116, bf16[4,4,128,256]{3,2,1,0:T(8,128)(2,1)} %get-tuple-element.508, ...), kind=kOutput, calls=%fused_computation.11.clone.1 | convolution fusion | flops 270532096 | bytes 4475424 | tf_op jit(solution)/shard_map/while/body/eval_jaxpr/gbd,gscd->gbsc/dot_general | solution.py:47
  86.0 0.8 exponential_reduce_fusion.2
  86.8 5.2 %all-gather = f32[16,4,128]{2,1,0:T(4,128)S(1)} all-gather(f32[4,4,128]{2,1,0:T(4,128)S(1)} %get-tuple-element.235), channel_id=2, replica_groups=mesh['imp'=8,'camp'=4] {'camp'}, dimensions={0}, use_global_device_ids=true | all-gather | bytes 40960 | tf_op jit(solution)/shard_map/all_gather | solution.py:13
  92.0 5.2 %all-gather.1 = f32[16,4,128]{2,1,0:T(4,128)S(1)} all-gather(f32[4,4,128]{2,1,0:T(4,128)S(1)} %get-tuple-element.236), channel_id=3, replica_groups=mesh['imp'=8,'camp'=4] {'camp'}, dimensions={0}, use_global_device_ids=true | all-gather | bytes 40960 | tf_op jit(solution)/shard_map/all_gather | solution.py:13
  97.2 0.1 while.41
  97.3 14.7 %while.42 = (s32[]{:T(128)}, f32[8,128]{1,0:T(8,128)S(1)}, s32[4,4,8]{2,1,0:T(4,128)S(1)}, s32[4,4]{1,0:T(4,128)S(1)}, bf16[4,4,128,256]{3,2,1,0:T(8,128)(2,1)},...) while((s32[]{:T(128)}, f32[8,128]{1,0:T(8,128)S(1)}, ...), condition=%wide.region_8.9_spmd.clone, body=%wide.region_6.8_spmd.clone.sunk | while | flops 272498304 | bytes 6668323 | solution.py:84
  97.5 0.7 gather_fusion.2
  98.2 0.6 gather_fusion.3
  98.8 2.0 %multiply_reduce_fusion.2 = f32[4,8,128]{2,1,0:T(8,128)S(1)} fusion(bf16[4,8,128,256]{3,2,1,0:T(8,128)(2,1)S(1)} %bitcast.115, f32[4,128]{1,0:T(4,128)S(1)} %get-tuple-element.484, f32[4,128]{1,0:T(4,128)S(1)} %get-tuple-element.485, f32[4,128]{1,0:T(4,128)S(1)} %dynamic-slice_bitcast_fusion.8, f32[4,8,128]{2,1,0:T(8,128)S(1)} %bitcast.121, ...), kind=kOutput, calls=%fused_computation.24.clone.1 | convolution fusion | flops 272101376 | bytes 2398752 | tf_op jit(solution)/shard_map/while/body/eval_jaxpr/gbd,gscd->gbsc/dot_general | solution.py:47
  100.8 0.2 fusion.38
  101.1 0.7 gather_fusion.2
  101.8 0.6 gather_fusion.3
  102.5 2.0 %multiply_reduce_fusion.2 = f32[4,8,128]{2,1,0:T(8,128)S(1)} fusion(bf16[4,8,128,256]{3,2,1,0:T(8,128)(2,1)S(1)} %bitcast.115, f32[4,128]{1,0:T(4,128)S(1)} %get-tuple-element.484, f32[4,128]{1,0:T(4,128)S(1)} %get-tuple-element.485, f32[4,128]{1,0:T(4,128)S(1)} %dynamic-slice_bitcast_fusion.8, f32[4,8,128]{2,1,0:T(8,128)S(1)} %bitcast.121, ...), kind=kOutput, calls=%fused_computation.24.clone.1 | convolution fusion | flops 272101376 | bytes 2398752 | tf_op jit(solution)/shard_map/while/body/eval_jaxpr/gbd,gscd->gbsc/dot_general | solution.py:47
  104.5 0.2 fusion.38
  104.8 0.7 gather_fusion.2
  105.5 0.6 gather_fusion.3
  106.2 2.0 %multiply_reduce_fusion.2 = f32[4,8,128]{2,1,0:T(8,128)S(1)} fusion(bf16[4,8,128,256]{3,2,1,0:T(8,128)(2,1)S(1)} %bitcast.115, f32[4,128]{1,0:T(4,128)S(1)} %get-tuple-element.484, f32[4,128]{1,0:T(4,128)S(1)} %get-tuple-element.485, f32[4,128]{1,0:T(4,128)S(1)} %dynamic-slice_bitcast_fusion.8, f32[4,8,128]{2,1,0:T(8,128)S(1)} %bitcast.121, ...), kind=kOutput, calls=%fused_computation.24.clone.1 | convolution fusion | flops 272101376 | bytes 2398752 | tf_op jit(solution)/shard_map/while/body/eval_jaxpr/gbd,gscd->gbsc/dot_general | solution.py:47
  108.2 0.2 fusion.38
  108.5 0.7 gather_fusion.2
  109.2 0.6 gather_fusion.3
  109.9 2.0 %multiply_reduce_fusion.2 = f32[4,8,128]{2,1,0:T(8,128)S(1)} fusion(bf16[4,8,128,256]{3,2,1,0:T(8,128)(2,1)S(1)} %bitcast.115, f32[4,128]{1,0:T(4,128)S(1)} %get-tuple-element.484, f32[4,128]{1,0:T(4,128)S(1)} %get-tuple-element.485, f32[4,128]{1,0:T(4,128)S(1)} %dynamic-slice_bitcast_fusion.8, f32[4,8,128]{2,1,0:T(8,128)S(1)} %bitcast.121, ...), kind=kOutput, calls=%fused_computation.24.clone.1 | convolution fusion | flops 272101376 | bytes 2398752 | tf_op jit(solution)/shard_map/while/body/eval_jaxpr/gbd,gscd->gbsc/dot_general | solution.py:47
  111.9 0.2 fusion.38
  112.1 30.6 %all-gather.4 = f32[8,1,1024]{2,1,0:T(1,128)S(1)} all-gather(f32[1,1,1024]{2,1,0:T(1,128)S(1)} %bitcast.125), channel_id=1, replica_groups=mesh['imp'=8,'camp'=4] {'imp'}, dimensions={0}, use_global_device_ids=true | all-gather | bytes 36864 | tf_op jit(solution)/shard_map/all_gather | solution.py:89
  142.7 0.6 log_add_fusion
  143.3 0.6 divide_add_fusion
  (74 shorter events, 1.9 us)
Async XLA Ops:
  7.2 63.1 %all-gather.7.cloned.1.call-start = ((), (), s32[]{:S(2)}) async-start(), calls=%async_computation | async-start | bytes 1310720 | tf_op jit(solution)/shard_map/all_gather | solution.py:25
  97.3 46.0 %copy-start = (bf16[128]{0:T(256)(128)(2,1)S(1)}, bf16[128]{0:T(256)(128)(2,1)}, u32[]{:S(2)}) copy-start(bf16[128]{0:T(256)(128)(2,1)} %param.16) | copy-start | bytes 772
  97.3 46.0 %copy-start.1 = (f32[128]{0:T(128)S(1)}, f32[128]{0:T(128)}, u32[]{:S(2)}) copy-start(f32[128]{0:T(128)} %param.17) | copy-start | bytes 1540
Sparse Core Ops, SparseCore 0:
  9.5 19.4 all-gather.6
